TPU v7x, 32 devices: a whole 2x2x4 slice. The times are simulated.
32 devices in a mesh: section: 4 (over z), seq: 8 (over y, x, core).
Axes of the slice: x: 2, y: 2, z: 4, core: 2. Of those that a mesh axis runs over, the one named last changes fastest.
Arguments:
- queries: bfloat16 [4, 2, 1024, 4096], P('section', None, 'seq'), may hold values from -80 to 80
- keys_new: bfloat16 [4, 2, 1024, 1024], P('section', None, 'seq'), may hold values from -4 to 4
- values_new: bfloat16 [4, 2, 1024, 1024], P('section', None, 'seq'), may hold values from -6 to 6
- key_cache: bfloat16 [4, 32, 4096, 128], P('section', 'seq'), may hold values from -6 to 6
- value_cache: bfloat16 [4, 32, 4096, 128], P('section', 'seq'), may hold values from -6 to 6
- block_lists: int32 [4, 32, 2, 16, 32], P('section', 'seq'), may hold values from 0 to 63, as said below
- block_counts: int32 [4, 32, 2, 16], P('section', 'seq'), may hold values from 1 to 32
- visible_blocks: int32 [2], replicated, may hold values from 32 to 64
Outputs:
- handed: bfloat16 [4, 2, 1024, 4096], P('section', None, 'seq')
Inputs may be any that keep to these rules, and one draw needn't show every extreme that they name: `block_lists`: each list holds 32 different block numbers.
All inputs are finite; a program needn't handle non-finite values.
Results may differ from a plain program's by a relative error of at most 0.003.
Values may be sent and summed in bfloat16 or wider, within the bound.
A program may use at most 192 MiB of HBM per device.

v0:
```python
import functools
import math

import jax
import jax.numpy as jnp
from jax import lax
from jax.experimental import pallas as pl
from jax.experimental.pallas import tpu as pltpu
from jax.sharding import PartitionSpec as P

HEADS = 32
KVH = 8
DH = 128
BLK = 64
GROUP = HEADS // KVH
ROW_TILE = 256
CHUNK = 4
TASKS = 4


def mesh_copy(src, dst, send_sem, recv_sem, section, seq):
    return pltpu.make_async_remote_copy(
        src_ref=src,
        dst_ref=dst,
        send_sem=send_sem,
        recv_sem=recv_sem,
        device_id=(section, seq),
        device_id_type=pl.DeviceIdType.MESH,
    )


def scores_of(query, keys):
    return lax.dot_general(
        query, keys, (((1,), (1,)), ((), ())), preferred_element_type=jnp.float32
    )


def fused(
    n,
    sections,
    lists,
    biases,
    queries,
    keys_new,
    values_new,
    key_cache,
    value_cache,
    out,
    qbuf,
    kbuf,
    vbuf,
    ckeys,
    cvalues,
    att,
    own_max,
    own_sum,
    own_out,
    in_send,
    in_recv,
    in_local,
    cache_sem,
    out_send,
    out_recv,
):
    spans, heads, span_len = qbuf.shape[0], qbuf.shape[1], qbuf.shape[2]
    kv_dev = kbuf.shape[1]
    rows = queries.shape[2]
    slots = lists.shape[1]
    query_blocks = span_len // BLK
    items = 2 * kv_dev + heads
    weight_scale = math.log2(math.e) / math.sqrt(DH)
    section = lax.axis_index("section")
    me = lax.axis_index("seq")
    above = lax.rem(section + 1, sections)
    below = lax.rem(section + sections - 1, sections)

    for head in range(heads):
        pltpu.make_async_copy(key_cache.at[0, head], ckeys.at[head], cache_sem.at[0, head]).start()
        pltpu.make_async_copy(
            value_cache.at[0, head], cvalues.at[head], cache_sem.at[1, head]
        ).start()

    def source(span, item, seq):
        if isinstance(item, int) and item < 2 * kv_dev:
            array = keys_new if item < kv_dev else values_new
            column = lax.div(seq * heads, GROUP) * DH + (item % kv_dev) * DH
        else:
            array = queries
            column = (seq * heads + item - 2 * kv_dev) * DH
        return array.at[0, span, :, pl.ds(pl.multiple_of(column, DH), DH)]

    def landing(span, item, seq):
        where = pl.ds(pl.multiple_of(seq * rows, rows), rows)
        if isinstance(item, int) and item < kv_dev:
            return kbuf.at[span, item, where, :]
        if isinstance(item, int) and item < 2 * kv_dev:
            return vbuf.at[span, item - kv_dev, where, :]
        return qbuf.at[span, item - 2 * kv_dev, where, :]

    def own_copy(span, item):
        return pltpu.make_async_copy(
            source(span, item, me), landing(span, item, me), in_local.at[span, item]
        )

    for span in range(spans):
        for item in range(items):
            own_copy(span, item).start()

    barrier = pltpu.get_barrier_semaphore()

    def greet(k, carry):
        @pl.when(k > 0)
        def _():
            pl.semaphore_signal(
                barrier,
                inc=1,
                device_id=(section, lax.rem(me + k, n)),
                device_id_type=pl.DeviceIdType.MESH,
            )

        for there in (above, below):
            pl.semaphore_signal(
                barrier,
                inc=1,
                device_id=(there, lax.rem(me + k, n)),
                device_id_type=pl.DeviceIdType.MESH,
            )
        return carry

    lax.fori_loop(0, n, greet, 0)
    pl.semaphore_wait(barrier, 3 * n - 1)

    def in_copy(span, item, k, seq_to, seq_from):
        return mesh_copy(
            source(span, item, seq_to),
            landing(span, item, seq_from),
            in_send.at[span, item, k],
            in_recv.at[span, item, k],
            section,
            seq_to,
        )

    for span in range(spans):
        for item in range(items):

            def send_in(k, carry):
                in_copy(span, item, k, lax.rem(me + k, n), me).start()
                return carry

            lax.fori_loop(1, n, send_in, 0)

    def await_in(span, item):
        own_copy(span, item).wait()

        def one(k, carry):
            in_copy(
                span, item, k, lax.rem(me + k, n), lax.rem(me + n - k, n)
            ).wait_recv()
            return carry

        lax.fori_loop(1, n, one, 0)

    def out_copy(span, head, k, seq_to, seq_from):
        column = pl.multiple_of((seq_from * heads + head) * DH, DH)
        return mesh_copy(
            att.at[span, head, pl.ds(pl.multiple_of(seq_to * rows, rows), rows), :],
            out.at[0, span, :, pl.ds(column, DH)],
            out_send.at[span, head, k],
            out_recv.at[span, head, k],
            above,
            seq_to,
        )

    row_at = lax.broadcasted_iota(jnp.int32, (ROW_TILE, ROW_TILE), 0)
    key_at = lax.broadcasted_iota(jnp.int32, (ROW_TILE, ROW_TILE), 1)

    def weigh(scores, top):
        return jnp.exp2((scores - top) * weight_scale)

    def own_part(span, head, kv, tile):
        start = tile * ROW_TILE
        query = qbuf[span, head, start : start + ROW_TILE, :]
        parts = []
        for piece in range(tile + 1):
            keys = kbuf[span, kv, piece * ROW_TILE : (piece + 1) * ROW_TILE, :]
            scores = scores_of(query, keys)
            if piece == tile:
                scores = jnp.where(row_at >= key_at, scores, -jnp.inf)
            parts.append(scores)
        top = jnp.max(functools.reduce(jnp.maximum, parts), axis=1, keepdims=True)
        summed, mixed = None, None
        for piece, scores in enumerate(parts):
            weights = weigh(scores, top)
            values = vbuf[span, kv, piece * ROW_TILE : (piece + 1) * ROW_TILE, :]
            product = jnp.dot(
                weights.astype(jnp.bfloat16), values, preferred_element_type=jnp.float32
            )
            summed = weights if summed is None else summed + weights
            mixed = product if mixed is None else mixed + product
        total = jnp.sum(summed, axis=1, keepdims=True)
        own_max[start : start + ROW_TILE, :] = jnp.broadcast_to(top, (ROW_TILE, DH))
        own_sum[start : start + ROW_TILE, :] = jnp.broadcast_to(total, (ROW_TILE, DH))
        own_out[start : start + ROW_TILE, :] = mixed

    def cache_part(span, head, block):
        listed = (head * spans + span) * query_blocks + block
        at = pl.ds(pl.multiple_of(block * BLK, BLK), BLK)
        query = qbuf[span, head, at, :]
        chosen = [lists[listed, i] for i in range(slots)]
        bias = biases[listed]
        parts = []
        for first in range(0, slots, CHUNK):
            keys = jnp.concatenate(
                [
                    ckeys[head, chosen[i]]
                    for i in range(first, first + CHUNK)
                ],
                axis=0,
            )
            scores = scores_of(query, keys)
            parts.append(scores + bias[first // CHUNK : first // CHUNK + 1, :])
        before = own_max[at, :][:, :1]
        top = jnp.max(functools.reduce(jnp.maximum, parts), axis=1, keepdims=True)
        top = jnp.maximum(top, before)
        summed, mixed = None, None
        for step, scores in enumerate(parts):
            weights = weigh(scores, top)
            values = jnp.concatenate(
                [
                    cvalues[head, chosen[i]]
                    for i in range(step * CHUNK, (step + 1) * CHUNK)
                ],
                axis=0,
            )
            product = jnp.dot(
                weights.astype(jnp.bfloat16), values, preferred_element_type=jnp.float32
            )
            summed = weights if summed is None else summed + weights
            mixed = product if mixed is None else mixed + product
        fade = weigh(before, top)
        total = jnp.sum(summed, axis=1, keepdims=True) + own_sum[at, :][:, :1] * fade
        return ((mixed + own_out[at, :] * fade) / total).astype(jnp.bfloat16)

    for head in range(heads):
        pltpu.make_async_copy(key_cache.at[0, head], ckeys.at[head], cache_sem.at[0, head]).wait()
        pltpu.make_async_copy(
            value_cache.at[0, head], cvalues.at[head], cache_sem.at[1, head]
        ).wait()

    for span in range(spans):
        for item in range(2 * kv_dev):
            await_in(span, item)

        def one_head(head, carry):
            kv = lax.div(head, GROUP)
            await_in(span, 2 * kv_dev + head)
            for tile in range(span_len // ROW_TILE):
                own_part(span, head, kv, tile)

            def tasks(step, inner):
                done = [cache_part(span, head, step * TASKS + t) for t in range(TASKS)]
                for t in range(TASKS):
                    at = pl.ds(pl.multiple_of((step * TASKS + t) * BLK, BLK), BLK)
                    att[span, head, at, :] = done[t]
                return inner

            lax.fori_loop(0, query_blocks // TASKS, tasks, 0)

            def send_out(k, inner):
                out_copy(span, head, k, lax.rem(me + k, n), me).start()
                return inner

            lax.fori_loop(0, n, send_out, 0)
            return carry

        lax.fori_loop(0, heads, one_head, 0)

    for span in range(spans):
        for item in range(items):

            def sent(k, carry):
                in_copy(span, item, k, lax.rem(me + k, n), me).wait_send()
                return carry

            lax.fori_loop(1, n, sent, 0)

        def head_done(head, carry):
            def both(k, inner):
                out_copy(span, head, k, lax.rem(me + k, n), me).wait_send()
                out_copy(
                    span, head, k, lax.rem(me + k, n), lax.rem(me + n - k, n)
                ).wait_recv()
                return inner

            return lax.fori_loop(0, n, both, carry)

        lax.fori_loop(0, heads, head_done, 0)


def on_device(
    queries, keys_new, values_new, key_cache, value_cache, block_lists, block_counts, visible_blocks
):
    n = lax.axis_size("seq")
    sections = lax.axis_size("section")
    spans, rows = queries.shape[1], queries.shape[2]
    heads, context = key_cache.shape[1], key_cache.shape[2]
    kv_dev = max(1, heads // GROUP)
    span_len = rows * n
    items = 2 * kv_dev + heads
    slots = block_lists.shape[4]
    smem = pl.BlockSpec(memory_space=pltpu.MemorySpace.SMEM)
    vmem = pl.BlockSpec(memory_space=pltpu.MemorySpace.VMEM)
    anywhere = pl.BlockSpec(memory_space=pl.ANY)
    usable = (jnp.arange(slots) < block_counts[0][..., None]) & (
        block_lists[0] < visible_blocks[None, :, None, None]
    )
    biases = jnp.where(usable, 0.0, -jnp.inf).astype(jnp.float32)
    biases = jnp.repeat(biases, BLK, axis=3).reshape(-1, slots // CHUNK, CHUNK * BLK)
    dma = pltpu.SemaphoreType.DMA
    return pl.pallas_call(
        functools.partial(fused, n, sections),
        out_shape=jax.ShapeDtypeStruct(queries.shape, queries.dtype),
        in_specs=[smem, vmem] + [anywhere] * 5,
        out_specs=anywhere,
        scratch_shapes=[
            pltpu.VMEM((spans, heads, span_len, DH), jnp.bfloat16),
            pltpu.VMEM((spans, kv_dev, span_len, DH), jnp.bfloat16),
            pltpu.VMEM((spans, kv_dev, span_len, DH), jnp.bfloat16),
            pltpu.VMEM((heads, context // BLK, BLK, DH), jnp.bfloat16),
            pltpu.VMEM((heads, context // BLK, BLK, DH), jnp.bfloat16),
            pltpu.VMEM((spans, heads, span_len, DH), jnp.bfloat16),
            pltpu.VMEM((span_len, DH), jnp.float32),
            pltpu.VMEM((span_len, DH), jnp.float32),
            pltpu.VMEM((span_len, DH), jnp.float32),
            dma((spans, items, n)),
            dma((spans, items, n)),
            dma((spans, items)),
            dma((2, heads)),
            dma((spans, heads, n)),
            dma((spans, heads, n)),
        ],
        compiler_params=pltpu.CompilerParams(
            collective_id=0, has_side_effects=True, vmem_limit_bytes=60 << 20
        ),
    )(
        block_lists.reshape(-1, slots),
        biases,
        queries,
        keys_new,
        values_new,
        key_cache.reshape(1, heads, context // BLK, BLK, DH),
        value_cache.reshape(1, heads, context // BLK, BLK, DH),
    )


def solution(mesh):
    return jax.shard_map(
        on_device,
        mesh=mesh,
        in_specs=(
            P("section", None, "seq", None),
            P("section", None, "seq", None),
            P("section", None, "seq", None),
            P("section", "seq", None, None),
            P("section", "seq", None, None),
            P("section", "seq", None, None, None),
            P("section", "seq", None, None),
            P(),
        ),
        out_specs=P("section", None, "seq", None),
        check_vma=False,
    )
```

profile of v0, /device:TPU:0, one launch (start us, length us, event | category | flops | bytes accessed | tf_op | source)
XLA Modules:
  0.0 126.1 jit_solution(10153283103618306509)
XLA Ops:
  0.0 0.9 fusion.1
  0.9 0.6 broadcast_in_dim.15
  1.6 1.5 %reshape_reshape.3.biases = f32[128,8,256]{2,1,0:T(8,128)} reshape(f32[4,2,16,32,64]{4,3,2,1,0:T(8,128)S(1)} %broadcast_in_dim.15) | data formatting | bytes 2097152 | tf_op jit(solution)/shard_map/reshape;reshape | solution.py:318
  3.1 119.8 %shard_map.82 = bf16[1,2,128,4096]{3,2,1,0:T(8,128)(2,1)} custom-call(s32[128,32]{1,0:T(8,128)} %bitcast.12, f32[128,8,256]{2,1,0:T(8,128)} %reshape_reshape.3.biases, bf16[1,2,128,4096]{3,2,1,0:T(8,128)(2,1)} %queries.1, bf16[1,2,128,1024]{3,2,1,0:T(8,128)(2,1)} %keys_new.1, bf16[1,2,128,1024]{3,2,1,0:T(8,128)(2,1)} %values_new.1, ...), custom_call_target="tpu_custom_call" | custom-call | tf_op jit(solution)/shard_map/pallas_call | solution.py:320
  122.9 3.1 %copy.10 = bf16[1,2,128,4096]{3,2,1,0:T(8,128)(2,1)} copy(bf16[1,2,128,4096]{3,2,1,0:T(8,128)(2,1)} %shard_map.82) | data formatting | bytes 4194304
where the time goes:
time: 126 us
  Pallas kernels  120 us (95%)
  local copies, waits for them, and re-layouts  5.24 us (4%)
    pallas_call x1, Pallas kernels, on_device(): pl.pallas_call(functools.partial(fused, n, sections), out_shape=jax.Shape...  120 us
    unnamed x1, local copies, waits for them, and re-layouts  3.13 us

commit v1 on v0

v1 whole, which is shorter than its diff:
```python
import functools
import math

import jax
import jax.numpy as jnp
from jax import lax
from jax.experimental import pallas as pl
from jax.experimental.pallas import tpu as pltpu
from jax.sharding import PartitionSpec as P

DH = 128
BLK = 64
GROUP = 4
LANES = 128
ROW_TILE = 256
CHUNK = 512
FAR = -1e30


def mesh_copy(src, dst, send_sem, recv_sem, section, seq):
    return pltpu.make_async_remote_copy(
        src_ref=src,
        dst_ref=dst,
        send_sem=send_sem,
        recv_sem=recv_sem,
        device_id=(section, seq),
        device_id_type=pl.DeviceIdType.MESH,
    )


def scores_of(query, keys):
    return lax.dot_general(
        query, keys, (((1,), (1,)), ((), ())), preferred_element_type=jnp.float32
    )


def whole_max(best, scores):
    for i in range(0, scores.shape[1], LANES):
        part = scores[:, i : i + LANES]
        best = part if best is None else jnp.maximum(best, part)
    return best


def fused(
    n,
    sections,
    visible,
    lists,
    counts,
    queries,
    keys_new,
    values_new,
    key_cache,
    value_cache,
    out,
    qbuf,
    kbuf,
    vbuf,
    ckeys,
    cvalues,
    reach,
    att,
    score_buf,
    top_buf,
    in_send,
    in_recv,
    in_local,
    cache_sem,
    out_send,
    out_recv,
):
    spans, heads, span_len = qbuf.shape[0], qbuf.shape[1], qbuf.shape[2]
    context = ckeys.shape[1]
    kv_dev = kbuf.shape[1]
    rows = queries.shape[2]
    slots = lists.shape[1]
    query_blocks = span_len // BLK
    items = 2 * kv_dev + heads
    tiles = span_len // ROW_TILE
    columns = reach.shape[1]
    weight_scale = math.log2(math.e) / math.sqrt(DH)
    section = lax.axis_index("section")
    me = lax.axis_index("seq")
    above = lax.rem(section + 1, sections)
    below = lax.rem(section + sections - 1, sections)

    def key_copy(head):
        return pltpu.make_async_copy(key_cache.at[0, head], ckeys.at[head], cache_sem.at[0, head])

    def value_copy(head):
        return pltpu.make_async_copy(
            value_cache.at[0, head], cvalues.at[head], cache_sem.at[1, head]
        )

    def source(span, item, seq):
        if isinstance(item, int) and item < 2 * kv_dev:
            array = keys_new if item < kv_dev else values_new
            column = lax.div(seq * heads, GROUP) * DH + (item % kv_dev) * DH
        else:
            array = queries
            column = (seq * heads + item - 2 * kv_dev) * DH
        return array.at[0, span, :, pl.ds(pl.multiple_of(column, DH), DH)]

    def landing(span, item, seq):
        where = pl.ds(pl.multiple_of(seq * rows, rows), rows)
        if isinstance(item, int) and item < kv_dev:
            return kbuf.at[span, item, where, :]
        if isinstance(item, int) and item < 2 * kv_dev:
            return vbuf.at[span, item - kv_dev, where, :]
        return qbuf.at[span, item - 2 * kv_dev, where, :]

    def own_copy(span, item):
        return pltpu.make_async_copy(
            source(span, item, me), landing(span, item, me), in_local.at[span, item]
        )

    for span in range(spans):
        for item in range(items):
            own_copy(span, item).start()

    barrier = pltpu.get_barrier_semaphore()

    def greet(k, carry):
        @pl.when(k > 0)
        def _():
            pl.semaphore_signal(
                barrier,
                inc=1,
                device_id=(section, lax.rem(me + k, n)),
                device_id_type=pl.DeviceIdType.MESH,
            )

        for there in (above, below):
            pl.semaphore_signal(
                barrier,
                inc=1,
                device_id=(there, lax.rem(me + k, n)),
                device_id_type=pl.DeviceIdType.MESH,
            )
        return carry

    lax.fori_loop(0, n, greet, 0)
    pl.semaphore_wait(barrier, 3 * n - 1)

    for head in range(heads):
        key_copy(head).start()
        value_copy(head).start()

    def in_copy(span, item, k, seq_to, seq_from):
        return mesh_copy(
            source(span, item, seq_to),
            landing(span, item, seq_from),
            in_send.at[span, item, k],
            in_recv.at[span, item, k],
            section,
            seq_to,
        )

    for span in range(spans):
        for item in range(items):

            def send_in(k, carry):
                in_copy(span, item, k, lax.rem(me + k, n), me).start()
                return carry

            lax.fori_loop(1, n, send_in, 0)

    def await_in(span, item):
        own_copy(span, item).wait()

        def one(k, carry):
            in_copy(
                span, item, k, lax.rem(me + k, n), lax.rem(me + n - k, n)
            ).wait_recv()
            return carry

        lax.fori_loop(1, n, one, 0)

    def out_copy(span, head, k, seq_to, seq_from):
        column = pl.multiple_of((seq_from * heads + head) * DH, DH)
        return mesh_copy(
            att.at[span, head, pl.ds(pl.multiple_of(seq_to * rows, rows), rows), :],
            out.at[0, span, :, pl.ds(column, DH)],
            out_send.at[span, head, k],
            out_recv.at[span, head, k],
            above,
            seq_to,
        )

    def build_reach():
        lane = lax.broadcasted_iota(jnp.int32, (1, columns), 1)
        group = lax.div(lane, query_blocks)
        count = jnp.zeros((1, columns), jnp.float32)
        place = lax.rem(lax.broadcasted_iota(jnp.int32, (query_blocks, columns), 1), query_blocks)
        spread = jnp.where(
            place == lax.broadcasted_iota(jnp.int32, (query_blocks, columns), 0), 1.0, 0.0
        ).astype(jnp.bfloat16)
        span_at = lax.broadcasted_iota(jnp.int32, (spans, columns), 0)
        group_at = lax.div(lax.broadcasted_iota(jnp.int32, (spans, columns), 1), query_blocks)
        for head in range(heads):
            wide = jnp.dot(
                counts[0, head].astype(jnp.float32).astype(jnp.bfloat16),
                spread,
                preferred_element_type=jnp.float32,
            )
            wide = jnp.where(group_at == head * spans + span_at, wide, 0.0)
            count = count + jnp.sum(wide, axis=0, keepdims=True)
        seen = jnp.zeros((1, columns), jnp.int32)
        for span in range(spans):
            seen = jnp.where(lax.rem(group, spans) == span, visible[span], seen)
        seen = seen.astype(jnp.float32)
        eye = jnp.where(
            lax.broadcasted_iota(jnp.int32, (slots, slots), 0)
            == lax.broadcasted_iota(jnp.int32, (slots, slots), 1),
            1.0,
            0.0,
        ).astype(jnp.bfloat16)
        listed = lists[...].astype(jnp.float32)
        if columns > listed.shape[0]:
            listed = jnp.concatenate(
                [listed, jnp.zeros((columns - listed.shape[0], slots), jnp.float32)], axis=0
            )
        listed = scores_of(eye, listed.astype(jnp.bfloat16))
        slot = lax.broadcasted_iota(jnp.int32, (slots, columns), 0).astype(jnp.float32)
        listed = jnp.where((slot < count) & (listed < seen), listed, -1.0)
        blocks = context // BLK
        block = lax.broadcasted_iota(jnp.int32, (blocks, columns), 0).astype(jnp.float32)
        bias = jnp.full((blocks, columns), FAR, jnp.float32)
        for i in range(slots):
            bias = jnp.where(listed[i : i + 1, :] == block, 0.0, bias)
        for j in range(blocks):
            reach[j * BLK : (j + 1) * BLK, :] = jnp.broadcast_to(
                bias[j : j + 1, :], (BLK, columns)
            ).astype(jnp.bfloat16)

    build_reach()

    row_at = lax.broadcasted_iota(jnp.int32, (ROW_TILE, ROW_TILE), 0)
    key_at = lax.broadcasted_iota(jnp.int32, (ROW_TILE, ROW_TILE), 1)
    mark_row = lax.div(lax.broadcasted_iota(jnp.int32, (ROW_TILE, columns), 0), BLK)
    mark_lane = lax.broadcasted_iota(jnp.int32, (ROW_TILE, columns), 1)

    def score_steps(span, head, kv, tile):
        slot = tile % 2
        at = slice(tile * ROW_TILE, (tile + 1) * ROW_TILE)
        best = [None]
        first = (head * spans + span) * query_blocks + tile * (ROW_TILE // BLK)

        def keep(scores, start):
            score_buf[slot, :, start : start + scores.shape[1]] = scores
            best[0] = whole_max(best[0], scores)

        def cache(start):
            mark = jnp.where(mark_lane == mark_row + first, 1.0, 0.0).astype(jnp.bfloat16)
            query = jnp.concatenate([qbuf[span, head, at, :], mark], axis=1)
            keys = jnp.concatenate(
                [ckeys[head, start : start + CHUNK, :], reach[start : start + CHUNK, :]], axis=1
            )
            keep(scores_of(query, keys), start)

        def own(piece):
            keys = kbuf[span, kv, piece * ROW_TILE : (piece + 1) * ROW_TILE, :]
            scores = scores_of(qbuf[span, head, at, :], keys)
            if piece == tile:
                scores = jnp.where(row_at >= key_at, scores, FAR)
            keep(scores, context + piece * ROW_TILE)

        def finish():
            top = jnp.max(best[0], axis=1, keepdims=True)
            top_buf[slot] = jnp.broadcast_to(top, (ROW_TILE, LANES))

        return (
            [functools.partial(cache, start) for start in range(0, context, CHUNK)]
            + [functools.partial(own, piece) for piece in range(tile + 1)]
            + [finish]
        )

    def value_steps(span, head, kv, tile):
        slot = tile % 2
        total = [None]

        def part(start, values):
            top = top_buf[slot]
            size = values.shape[0]
            weights = []
            for i in range(start, start + size, LANES):
                scores = score_buf[slot, :, i : i + LANES]
                weights.append(jnp.exp2((scores - top) * weight_scale).astype(jnp.bfloat16))
            values = jnp.concatenate([values, jnp.ones((size, LANES), jnp.bfloat16)], axis=1)
            product = jnp.dot(
                jnp.concatenate(weights, axis=1), values, preferred_element_type=jnp.float32
            )
            total[0] = product if total[0] is None else total[0] + product

        def cache(start):
            part(start, cvalues[head, start : start + CHUNK, :])

        def own(piece):
            part(
                context + piece * ROW_TILE,
                vbuf[span, kv, piece * ROW_TILE : (piece + 1) * ROW_TILE, :],
            )

        def finish():
            mixed = total[0][:, :DH] / total[0][:, DH:]
            att[span, head, tile * ROW_TILE : (tile + 1) * ROW_TILE, :] = mixed.astype(
                jnp.bfloat16
            )

        return (
            [functools.partial(cache, start) for start in range(0, context, CHUNK)]
            + [functools.partial(own, piece) for piece in range(tile + 1)]
            + [finish]
        )

    def one_unit(unit, carry):
        span, head = lax.div(unit, heads), lax.rem(unit, heads)
        kv = lax.div(head, GROUP)

        @pl.when(head == 0)
        def _():
            for item in range(2 * kv_dev):
                await_in(span, item)

        @pl.when(span == 0)
        def _():
            key_copy(head).wait()
            value_copy(head).wait()

        await_in(span, 2 * kv_dev + head)
        for step in score_steps(span, head, kv, 0):
            step()
        for tile in range(tiles):
            now = value_steps(span, head, kv, tile)
            later = score_steps(span, head, kv, tile + 1) if tile + 1 < tiles else []
            for i in range(max(len(now), len(later))):
                if i < len(later):
                    later[i]()
                if i < len(now):
                    now[i]()

        def send_out(k, inner):
            out_copy(span, head, k, lax.rem(me + k, n), me).start()
            return inner

        lax.fori_loop(0, n, send_out, 0)
        return carry

    lax.fori_loop(0, spans * heads, one_unit, 0)

    for span in range(spans):
        for item in range(items):

            def sent(k, carry):
                in_copy(span, item, k, lax.rem(me + k, n), me).wait_send()
                return carry

            lax.fori_loop(1, n, sent, 0)

        def head_done(head, carry):
            def both(k, inner):
                out_copy(span, head, k, lax.rem(me + k, n), me).wait_send()
                out_copy(
                    span, head, k, lax.rem(me + k, n), lax.rem(me + n - k, n)
                ).wait_recv()
                return inner

            return lax.fori_loop(0, n, both, carry)

        lax.fori_loop(0, heads, head_done, 0)


def on_device(
    queries, keys_new, values_new, key_cache, value_cache, block_lists, block_counts, visible_blocks
):
    n = lax.axis_size("seq")
    sections = lax.axis_size("section")
    spans, rows = queries.shape[1], queries.shape[2]
    heads, context = key_cache.shape[1], key_cache.shape[2]
    kv_dev = max(1, heads // GROUP)
    span_len = rows * n
    items = 2 * kv_dev + heads
    slots = block_lists.shape[4]
    smem = pl.BlockSpec(memory_space=pltpu.MemorySpace.SMEM)
    vmem = pl.BlockSpec(memory_space=pltpu.MemorySpace.VMEM)
    anywhere = pl.BlockSpec(memory_space=pl.ANY)
    cols = -(-heads * spans * (span_len // BLK) // LANES) * LANES
    dma = pltpu.SemaphoreType.DMA
    return pl.pallas_call(
        functools.partial(fused, n, sections),
        out_shape=jax.ShapeDtypeStruct(queries.shape, queries.dtype),
        in_specs=[smem, vmem, vmem] + [anywhere] * 5,
        out_specs=anywhere,
        scratch_shapes=[
            pltpu.VMEM((spans, heads, span_len, DH), jnp.bfloat16),
            pltpu.VMEM((spans, kv_dev, span_len, DH), jnp.bfloat16),
            pltpu.VMEM((spans, kv_dev, span_len, DH), jnp.bfloat16),
            pltpu.VMEM((heads, context, DH), jnp.bfloat16),
            pltpu.VMEM((heads, context, DH), jnp.bfloat16),
            pltpu.VMEM((context, cols), jnp.bfloat16),
            pltpu.VMEM((spans, heads, span_len, DH), jnp.bfloat16),
            pltpu.VMEM((2, ROW_TILE, context + span_len), jnp.float32),
            pltpu.VMEM((2, ROW_TILE, LANES), jnp.float32),
            dma((spans, items, n)),
            dma((spans, items, n)),
            dma((spans, items)),
            dma((2, heads)),
            dma((spans, heads, n)),
            dma((spans, heads, n)),
        ],
        compiler_params=pltpu.CompilerParams(
            collective_id=0, has_side_effects=True, vmem_limit_bytes=60 << 20
        ),
    )(
        visible_blocks,
        block_lists.reshape(-1, slots),
        block_counts,
        queries,
        keys_new,
        values_new,
        key_cache,
        value_cache,
    )


def solution(mesh):
    return jax.shard_map(
        on_device,
        mesh=mesh,
        in_specs=(
            P("section", None, "seq", None),
            P("section", None, "seq", None),
            P("section", None, "seq", None),
            P("section", "seq", None, None),
            P("section", "seq", None, None),
            P("section", "seq", None, None, None),
            P("section", "seq", None, None),
            P(),
        ),
        out_specs=P("section", None, "seq", None),
        check_vma=False,
    )
```

time: 126 us -> 80.7 us (0.64)
  Pallas kernels: 120 us -> 77.4 us
  local copies, waits for them, and re-layouts: 5.24 us -> 3.13 us
    pallas_call x1, Pallas kernels: 120 us -> 77.4 us  [on_device(): pl.pallas_call(functools.partial(fused, n, sections), out_shape=jax.Shape...]
    another operation x1 -> x0, local copies, waits for them, and re-layouts: 1.51 us -> none  [on_device(): jnp.repeat(biases, BLK, axis=3).reshape(-1, slots // CHUNK, CHUNK * BLK)]
where the time goes in v1:
time: 80.7 us; the launch traced here: 80.5 us
  Pallas kernels  77.4 us (96%)
  local copies, waits for them, and re-layouts  3.13 us (4%)
    pallas_call x1, Pallas kernels, on_device(): pl.pallas_call(functools.partial(fused, n, sections), out_shape=jax.Shape...  77.4 us
    unnamed x1, local copies, waits for them, and re-layouts  3.13 us

profile of v1, /device:TPU:0, one launch (start us, length us, event | category | flops | bytes accessed | tf_op | source)
XLA Modules:
  0.0 80.5 jit_solution(10084288339039832469)
XLA Ops:
  0.0 77.4 %shard_map.82 = bf16[1,2,128,4096]{3,2,1,0:T(8,128)(2,1)} custom-call(s32[2]{0:T(128)} %visible.1, s32[128,32]{1,0:T(8,128)} %bitcast.1, s32[1,4,2,16]{3,2,1,0:T(2,128)} %counts.1, bf16[1,2,128,4096]{3,2,1,0:T(8,128)(2,1)} %queries.1, bf16[1,2,128,1024]{3,2,1,0:T(8,128)(2,1)} %keys_new.1, bf16[1,2,128,1024]{3,2,1,0:T(8,128)(2,1)} %values_new.1, ...), custom_call_target="tpu_custom_call" | custom-call | tf_op jit(solution)/shard_map/pallas_call | solution.py:389
  77.4 3.1 %copy.10 = bf16[1,2,128,4096]{3,2,1,0:T(8,128)(2,1)} copy(bf16[1,2,128,4096]{3,2,1,0:T(8,128)(2,1)} %shard_map.82) | data formatting | bytes 4194304

commit v2 on v1

--- a/solution.py
+++ b/solution.py
@@ -64,10 +64,10 @@
     top_buf,
     in_send,
     in_recv,
-    in_local,
     cache_sem,
     out_send,
     out_recv,
+    gate,
 ):
     spans, heads, span_len = qbuf.shape[0], qbuf.shape[1], qbuf.shape[2]
     context = ckeys.shape[1]
@@ -111,78 +111,83 @@
 
     def own_copy(span, item):
         return pltpu.make_async_copy(
-            source(span, item, me), landing(span, item, me), in_local.at[span, item]
-        )
+            source(span, item, me), landing(span, item, me), in_recv.at[span, item]
+        )
+
+    def in_copy(span, item, k):
+        seq_to = lax.rem(me + k, n)
+        return mesh_copy(
+            source(span, item, seq_to),
+            landing(span, item, me),
+            in_send.at[span, item],
+            in_recv.at[span, item],
+            section,
+            seq_to,
+        )
+
+    def received(span, item, count):
+        where = pl.ds(0, count * rows)
+        if isinstance(item, int) and item < kv_dev:
+            return kbuf.at[span, item, where, :]
+        if isinstance(item, int) and item < 2 * kv_dev:
+            return vbuf.at[span, item - kv_dev, where, :]
+        return qbuf.at[span, item - 2 * kv_dev, where, :]
+
+    def await_in(span, item):
+        whole = received(span, item, n)
+        pltpu.make_async_copy(whole, whole, in_recv.at[span, item]).wait()
+
+    def await_sent(span, item):
+        most = received(span, item, n - 1)
+        pltpu.make_async_copy(most, most, in_send.at[span, item]).wait()
+
+    order = [2 * kv_dev] + list(range(2 * kv_dev)) + list(range(2 * kv_dev + 1, items))
 
     for span in range(spans):
-        for item in range(items):
+        for item in order:
             own_copy(span, item).start()
 
     barrier = pltpu.get_barrier_semaphore()
 
     def greet(k, carry):
-        @pl.when(k > 0)
-        def _():
-            pl.semaphore_signal(
-                barrier,
-                inc=1,
-                device_id=(section, lax.rem(me + k, n)),
-                device_id_type=pl.DeviceIdType.MESH,
-            )
-
-        for there in (above, below):
-            pl.semaphore_signal(
-                barrier,
-                inc=1,
-                device_id=(there, lax.rem(me + k, n)),
-                device_id_type=pl.DeviceIdType.MESH,
-            )
+        pl.semaphore_signal(
+            barrier,
+            inc=1,
+            device_id=(section, lax.rem(me + k, n)),
+            device_id_type=pl.DeviceIdType.MESH,
+        )
         return carry
 
-    lax.fori_loop(0, n, greet, 0)
-    pl.semaphore_wait(barrier, 3 * n - 1)
+    lax.fori_loop(1, n, greet, 0)
+    for there in (above, below):
+        pl.semaphore_signal(
+            barrier, inc=1, device_id=(there, me), device_id_type=pl.DeviceIdType.MESH
+        )
+    pl.semaphore_wait(barrier, n + 1)
+
+    for span in range(spans):
+        for item in order:
+
+            def send_in(k, carry):
+                in_copy(span, item, k).start()
+                return carry
+
+            lax.fori_loop(1, n, send_in, 0)
+
+    pl.semaphore_signal(gate, inc=1, device_id=(below, me), device_id_type=pl.DeviceIdType.MESH)
 
     for head in range(heads):
         key_copy(head).start()
         value_copy(head).start()
 
-    def in_copy(span, item, k, seq_to, seq_from):
-        return mesh_copy(
-            source(span, item, seq_to),
-            landing(span, item, seq_from),
-            in_send.at[span, item, k],
-            in_recv.at[span, item, k],
-            section,
-            seq_to,
-        )
-
-    for span in range(spans):
-        for item in range(items):
-
-            def send_in(k, carry):
-                in_copy(span, item, k, lax.rem(me + k, n), me).start()
-                return carry
-
-            lax.fori_loop(1, n, send_in, 0)
-
-    def await_in(span, item):
-        own_copy(span, item).wait()
-
-        def one(k, carry):
-            in_copy(
-                span, item, k, lax.rem(me + k, n), lax.rem(me + n - k, n)
-            ).wait_recv()
-            return carry
-
-        lax.fori_loop(1, n, one, 0)
-
-    def out_copy(span, head, k, seq_to, seq_from):
-        column = pl.multiple_of((seq_from * heads + head) * DH, DH)
+    def out_copy(span, head, k):
+        seq_to = lax.rem(me + k, n)
+        column = pl.multiple_of((me * heads + head) * DH, DH)
         return mesh_copy(
             att.at[span, head, pl.ds(pl.multiple_of(seq_to * rows, rows), rows), :],
             out.at[0, span, :, pl.ds(column, DH)],
-            out_send.at[span, head, k],
-            out_recv.at[span, head, k],
+            out_send.at[0],
+            out_recv.at[0],
             above,
             seq_to,
         )
@@ -234,6 +239,7 @@
             ).astype(jnp.bfloat16)
 
     build_reach()
+    pl.semaphore_wait(gate, 1)
 
     row_at = lax.broadcasted_iota(jnp.int32, (ROW_TILE, ROW_TILE), 0)
     key_at = lax.broadcasted_iota(jnp.int32, (ROW_TILE, ROW_TILE), 1)
@@ -340,7 +346,7 @@
                     now[i]()
 
         def send_out(k, inner):
-            out_copy(span, head, k, lax.rem(me + k, n), me).start()
+            out_copy(span, head, k).start()
             return inner
 
         lax.fori_loop(0, n, send_out, 0)
@@ -350,24 +356,9 @@
 
     for span in range(spans):
         for item in range(items):
-
-            def sent(k, carry):
-                in_copy(span, item, k, lax.rem(me + k, n), me).wait_send()
-                return carry
-
-            lax.fori_loop(1, n, sent, 0)
-
-        def head_done(head, carry):
-            def both(k, inner):
-                out_copy(span, head, k, lax.rem(me + k, n), me).wait_send()
-                out_copy(
-                    span, head, k, lax.rem(me + k, n), lax.rem(me + n - k, n)
-                ).wait_recv()
-                return inner
-
-            return lax.fori_loop(0, n, both, carry)
-
-        lax.fori_loop(0, heads, head_done, 0)
+            await_sent(span, item)
+    pltpu.make_async_copy(att, att, out_send.at[0]).wait()
+    pltpu.make_async_copy(out, out, out_recv.at[0]).wait()
 
 
 def on_device(
@@ -388,9 +379,9 @@
     dma = pltpu.SemaphoreType.DMA
     return pl.pallas_call(
         functools.partial(fused, n, sections),
-        out_shape=jax.ShapeDtypeStruct(queries.shape, queries.dtype),
+        out_shape=pltpu.VMEM(queries.shape, queries.dtype),
         in_specs=[smem, vmem, vmem] + [anywhere] * 5,
-        out_specs=anywhere,
+        out_specs=vmem,
         scratch_shapes=[
             pltpu.VMEM((spans, heads, span_len, DH), jnp.bfloat16),
             pltpu.VMEM((spans, kv_dev, span_len, DH), jnp.bfloat16),
@@ -401,12 +392,12 @@
             pltpu.VMEM((spans, heads, span_len, DH), jnp.bfloat16),
             pltpu.VMEM((2, ROW_TILE, context + span_len), jnp.float32),
             pltpu.VMEM((2, ROW_TILE, LANES), jnp.float32),
-            dma((spans, items, n)),
-            dma((spans, items, n)),
+            dma((spans, items)),
             dma((spans, items)),
             dma((2, heads)),
-            dma((spans, heads, n)),
-            dma((spans, heads, n)),
+            dma((1,)),
+            dma((1,)),
+            pltpu.SemaphoreType.REGULAR,
         ],
         compiler_params=pltpu.CompilerParams(
             collective_id=0, has_side_effects=True, vmem_limit_bytes=60 << 20

time: 80.7 us -> 75.5 us (0.936)
  Pallas kernels: 77.4 us -> 74 us
  local copies, waits for them, and re-layouts: 3.13 us -> 1.32 us
    pallas_call x1, Pallas kernels: 77.4 us -> 74 us  [on_device(): pl.pallas_call(functools.partial(fused, n, sections), out_shape=pltpu.VME...]
    unnamed x1, local copies, waits for them, and re-layouts: 3.13 us -> 1.32 us
where the time goes in v2:
time: 75.5 us; the launch traced here: 75.4 us
  Pallas kernels  74 us (98%)
  local copies, waits for them, and re-layouts  1.32 us (2%)
    pallas_call x1, Pallas kernels, on_device(): pl.pallas_call(functools.partial(fused, n, sections), out_shape=pltpu.VME...  74 us

profile of v2, /device:TPU:0, one launch (start us, length us, event | category | flops | bytes accessed | tf_op | source)
XLA Modules:
  0.0 75.4 jit_solution(16229257202797164750)
XLA Ops:
  0.0 74.0 %shard_map.82 = bf16[1,2,128,4096]{3,2,1,0:T(8,128)(2,1)S(1)} custom-call(s32[2]{0:T(128)} %visible.1, s32[128,32]{1,0:T(8,128)} %bitcast.1, s32[1,4,2,16]{3,2,1,0:T(2,128)} %counts.1, bf16[1,2,128,4096]{3,2,1,0:T(8,128)(2,1)} %queries.1, bf16[1,2,128,1024]{3,2,1,0:T(8,128)(2,1)} %keys_new.1, bf16[1,2,128,1024]{3,2,1,0:T(8,128)(2,1)} %values_new.1, ...), custom_call_target="tpu_custom_call" | custom-call | tf_op jit(solution)/shard_map/pallas_call | solution.py:380
  74.1 1.3 %copy.10 = bf16[1,2,128,4096]{3,2,1,0:T(8,128)(2,1)} copy(bf16[1,2,128,4096]{3,2,1,0:T(8,128)(2,1)S(1)} %shard_map.82) | data formatting | bytes 4194304

commit v3 on v2

--- a/solution.py
+++ b/solution.py
@@ -15,6 +15,8 @@
 ROW_TILE = 256
 CHUNK = 512
 FAR = -1e30
+DIRECT = 4
+LAG = 3
 
 
 def mesh_copy(src, dst, send_sem, recv_sem, section, seq):
@@ -67,6 +69,9 @@
     cache_sem,
     out_send,
     out_recv,
+    stage,
+    stage_recv,
+    pass_send,
     gate,
 ):
     spans, heads, span_len = qbuf.shape[0], qbuf.shape[1], qbuf.shape[2]
@@ -180,17 +185,50 @@
         key_copy(head).start()
         value_copy(head).start()
 
+    units = spans * heads
+    relayed = max(0, units - DIRECT)
+
+    def out_piece(buffer, span, head, seq_from, seq_to):
+        column = pl.multiple_of((seq_from * heads + head) * DH, DH)
+        where = pl.ds(pl.multiple_of(seq_to * rows, rows), rows)
+        return buffer.at[where, :], out.at[0, span, :, pl.ds(column, DH)]
+
     def out_copy(span, head, k):
         seq_to = lax.rem(me + k, n)
-        column = pl.multiple_of((me * heads + head) * DH, DH)
+        source_ref, target_ref = out_piece(att.at[span, head], span, head, me, seq_to)
+        return mesh_copy(source_ref, target_ref, out_send.at[0], out_recv.at[0], above, seq_to)
+
+    def up_copy(span, head, tile):
+        where = pl.ds(tile * ROW_TILE, ROW_TILE)
+        unit = span * heads + head
         return mesh_copy(
-            att.at[span, head, pl.ds(pl.multiple_of(seq_to * rows, rows), rows), :],
-            out.at[0, span, :, pl.ds(column, DH)],
+            att.at[span, head, where, :],
+            stage.at[unit, where, :],
             out_send.at[0],
-            out_recv.at[0],
+            stage_recv.at[unit],
             above,
-            seq_to,
-        )
+            me,
+        )
+
+    def pass_on(unit):
+        span, head = unit // heads, unit % heads
+        whole = stage.at[unit]
+        pltpu.make_async_copy(whole, whole, stage_recv.at[unit]).wait()
+        source_ref, target_ref = out_piece(whole, span, head, me, me)
+        pltpu.make_async_copy(source_ref, target_ref, out_recv.at[0]).start()
+
+        def one(k, carry):
+            seq_to = lax.rem(me + k, n)
+            source_ref, target_ref = out_piece(whole, span, head, me, seq_to)
+            mesh_copy(
+                source_ref, target_ref, pass_send.at[0], out_recv.at[0], section, seq_to
+            ).start()
+            return carry
+
+        lax.fori_loop(1, n, one, 0)
+
+    def pass_after(unit):
+        return max(unit + LAG, units // 2 - 1 + (unit > 0))
 
     def build_reach():
         lane = lax.broadcasted_iota(jnp.int32, (1, columns), 1)
@@ -345,19 +383,40 @@
                 if i < len(now):
                     now[i]()
 
-        def send_out(k, inner):
-            out_copy(span, head, k).start()
-            return inner
-
-        lax.fori_loop(0, n, send_out, 0)
+
+        @pl.when(unit < relayed)
+        def _():
+            for tile in range(tiles):
+                up_copy(span, head, tile).start()
+
+        @pl.when(unit >= relayed)
+        def _():
+            def send_out(k, inner):
+                out_copy(span, head, k).start()
+                return inner
+
+            lax.fori_loop(0, n, send_out, 0)
+
+        for done in range(relayed):
+
+            @pl.when(unit == pass_after(done))
+            def _():
+                pass_on(done)
+
         return carry
 
-    lax.fori_loop(0, spans * heads, one_unit, 0)
+    lax.fori_loop(0, units, one_unit, 0)
+    for done in range(relayed):
+        if pass_after(done) >= units:
+            pass_on(done)
 
     for span in range(spans):
         for item in range(items):
             await_sent(span, item)
     pltpu.make_async_copy(att, att, out_send.at[0]).wait()
+    if relayed:
+        passed = stage.at[:, pl.ds(0, (n - 1) * rows), :]
+        pltpu.make_async_copy(passed, passed, pass_send.at[0]).wait()
     pltpu.make_async_copy(out, out, out_recv.at[0]).wait()
 
 
@@ -375,6 +434,7 @@
     smem = pl.BlockSpec(memory_space=pltpu.MemorySpace.SMEM)
     vmem = pl.BlockSpec(memory_space=pltpu.MemorySpace.VMEM)
     anywhere = pl.BlockSpec(memory_space=pl.ANY)
+    relayed = max(0, spans * heads - DIRECT)
     cols = -(-heads * spans * (span_len // BLK) // LANES) * LANES
     dma = pltpu.SemaphoreType.DMA
     return pl.pallas_call(
@@ -397,6 +457,9 @@
             dma((2, heads)),
             dma((1,)),
             dma((1,)),
+            pltpu.VMEM((relayed, span_len, DH), jnp.bfloat16),
+            dma((relayed,)),
+            dma((1,)),
             pltpu.SemaphoreType.REGULAR,
         ],
         compiler_params=pltpu.CompilerParams(

time: 75.5 us -> 72.6 us (0.962)
  Pallas kernels: 74 us -> 71.1 us
    pallas_call x1, Pallas kernels: 74 us -> 71.1 us  [on_device(): pl.pallas_call(functools.partial(fused, n, sections), out_shape=pltpu.VME...]
where the time goes in v3:
time: 72.6 us; the launch traced here: 72.4 us
  Pallas kernels  71.1 us (98%)
  local copies, waits for them, and re-layouts  1.32 us (2%)
    pallas_call x1, Pallas kernels, on_device(): pl.pallas_call(functools.partial(fused, n, sections), out_shape=pltpu.VME...  71.1 us

profile of v3, /device:TPU:0, one launch (start us, length us, event | category | flops | bytes accessed | tf_op | source)
XLA Modules:
  0.0 72.4 jit_solution(9898394660473276797)
XLA Ops:
  0.0 71.1 %shard_map.82 = bf16[1,2,128,4096]{3,2,1,0:T(8,128)(2,1)S(1)} custom-call(s32[2]{0:T(128)} %visible.1, s32[128,32]{1,0:T(8,128)} %bitcast.1, s32[1,4,2,16]{3,2,1,0:T(2,128)} %counts.1, bf16[1,2,128,4096]{3,2,1,0:T(8,128)(2,1)} %queries.1, bf16[1,2,128,1024]{3,2,1,0:T(8,128)(2,1)} %keys_new.1, bf16[1,2,128,1024]{3,2,1,0:T(8,128)(2,1)} %values_new.1, ...), custom_call_target="tpu_custom_call" | custom-call | tf_op jit(solution)/shard_map/pallas_call | solution.py:440
  71.1 1.3 %copy.10 = bf16[1,2,128,4096]{3,2,1,0:T(8,128)(2,1)} copy(bf16[1,2,128,4096]{3,2,1,0:T(8,128)(2,1)S(1)} %shard_map.82) | data formatting | bytes 4194304

commit v4 on v3

--- a/solution.py
+++ b/solution.py
@@ -148,10 +148,6 @@
 
     order = [2 * kv_dev] + list(range(2 * kv_dev)) + list(range(2 * kv_dev + 1, items))
 
-    for span in range(spans):
-        for item in order:
-            own_copy(span, item).start()
-
     barrier = pltpu.get_barrier_semaphore()
 
     def greet(k, carry):
@@ -170,14 +166,19 @@
         )
     pl.semaphore_wait(barrier, n + 1)
 
-    for span in range(spans):
-        for item in order:
+    def send_items(span, some):
+        for item in some:
 
             def send_in(k, carry):
                 in_copy(span, item, k).start()
                 return carry
 
             lax.fori_loop(1, n, send_in, 0)
+        for item in some:
+            own_copy(span, item).start()
+
+    urgent = 1 + 2 * kv_dev
+    send_items(0, order[:urgent])
 
     pl.semaphore_signal(gate, inc=1, device_id=(below, me), device_id_type=pl.DeviceIdType.MESH)
 
@@ -186,7 +187,7 @@
         value_copy(head).start()
 
     units = spans * heads
-    relayed = max(0, units - DIRECT)
+    relayed = max(1, units - DIRECT)
 
     def out_piece(buffer, span, head, seq_from, seq_to):
         column = pl.multiple_of((seq_from * heads + head) * DH, DH)
@@ -228,7 +229,7 @@
         lax.fori_loop(1, n, one, 0)
 
     def pass_after(unit):
-        return max(unit + LAG, units // 2 - 1 + (unit > 0))
+        return max(1, unit + LAG, units // 2 - 1 + (unit > 0))
 
     def build_reach():
         lane = lax.broadcasted_iota(jnp.int32, (1, columns), 1)
@@ -285,7 +286,7 @@
     mark_lane = lax.broadcasted_iota(jnp.int32, (ROW_TILE, columns), 1)
 
     def score_steps(span, head, kv, tile):
-        slot = tile % 2
+        slot = tile
         at = slice(tile * ROW_TILE, (tile + 1) * ROW_TILE)
         best = [None]
         first = (head * spans + span) * query_blocks + tile * (ROW_TILE // BLK)
@@ -314,13 +315,12 @@
             top_buf[slot] = jnp.broadcast_to(top, (ROW_TILE, LANES))
 
         return (
-            [functools.partial(cache, start) for start in range(0, context, CHUNK)]
-            + [functools.partial(own, piece) for piece in range(tile + 1)]
-            + [finish]
+            [functools.partial(cache, start) for start in range(0, context, CHUNK)],
+            [functools.partial(own, piece) for piece in range(tile + 1)] + [finish],
         )
 
     def value_steps(span, head, kv, tile):
-        slot = tile % 2
+        slot = tile
         total = [None]
 
         def part(start, values):
@@ -357,6 +357,34 @@
             + [finish]
         )
 
+    def together(first, second):
+        for i in range(max(len(first), len(second))):
+            if i < len(first):
+                first[i]()
+            if i < len(second):
+                second[i]()
+
+    def first_unit():
+        key_copy(0).wait()
+        value_copy(0).wait()
+        await_in(0, 2 * kv_dev)
+        steps = [score_steps(0, 0, 0, tile) for tile in range(tiles)]
+        for cached, _ in steps:
+            for step in cached:
+                step()
+        send_items(0, order[urgent:])
+        for span in range(1, spans):
+            send_items(span, order)
+        for item in range(2 * kv_dev):
+            await_in(0, item)
+        for step in steps[0][1]:
+            step()
+        for tile in range(tiles):
+            later = steps[tile + 1][1] if tile + 1 < tiles else []
+            together(later, value_steps(0, 0, 0, tile))
+        for tile in range(tiles):
+            up_copy(0, 0, tile).start()
+
     def one_unit(unit, carry):
         span, head = lax.div(unit, heads), lax.rem(unit, heads)
         kv = lax.div(head, GROUP)
@@ -372,17 +400,14 @@
             value_copy(head).wait()
 
         await_in(span, 2 * kv_dev + head)
-        for step in score_steps(span, head, kv, 0):
-            step()
+        for steps in score_steps(span, head, kv, 0):
+            for step in steps:
+                step()
         for tile in range(tiles):
-            now = value_steps(span, head, kv, tile)
-            later = score_steps(span, head, kv, tile + 1) if tile + 1 < tiles else []
-            for i in range(max(len(now), len(later))):
-                if i < len(later):
-                    later[i]()
-                if i < len(now):
-                    now[i]()
-
+            later = []
+            if tile + 1 < tiles:
+                later = sum(score_steps(span, head, kv, tile + 1), [])
+            together(later, value_steps(span, head, kv, tile))
 
         @pl.when(unit < relayed)
         def _():
@@ -405,7 +430,8 @@
 
         return carry
 
-    lax.fori_loop(0, units, one_unit, 0)
+    first_unit()
+    lax.fori_loop(1, units, one_unit, 0)
     for done in range(relayed):
         if pass_after(done) >= units:
             pass_on(done)
@@ -414,9 +440,8 @@
         for item in range(items):
             await_sent(span, item)
     pltpu.make_async_copy(att, att, out_send.at[0]).wait()
-    if relayed:
-        passed = stage.at[:, pl.ds(0, (n - 1) * rows), :]
-        pltpu.make_async_copy(passed, passed, pass_send.at[0]).wait()
+    passed = stage.at[:, pl.ds(0, (n - 1) * rows), :]
+    pltpu.make_async_copy(passed, passed, pass_send.at[0]).wait()
     pltpu.make_async_copy(out, out, out_recv.at[0]).wait()
 
 
@@ -434,7 +459,8 @@
     smem = pl.BlockSpec(memory_space=pltpu.MemorySpace.SMEM)
     vmem = pl.BlockSpec(memory_space=pltpu.MemorySpace.VMEM)
     anywhere = pl.BlockSpec(memory_space=pl.ANY)
-    relayed = max(0, spans * heads - DIRECT)
+    relayed = max(1, spans * heads - DIRECT)
+    tiles = span_len // ROW_TILE
     cols = -(-heads * spans * (span_len // BLK) // LANES) * LANES
     dma = pltpu.SemaphoreType.DMA
     return pl.pallas_call(
@@ -450,8 +476,8 @@
             pltpu.VMEM((heads, context, DH), jnp.bfloat16),
             pltpu.VMEM((context, cols), jnp.bfloat16),
             pltpu.VMEM((spans, heads, span_len, DH), jnp.bfloat16),
-            pltpu.VMEM((2, ROW_TILE, context + span_len), jnp.float32),
-            pltpu.VMEM((2, ROW_TILE, LANES), jnp.float32),
+            pltpu.VMEM((tiles, ROW_TILE, context + span_len), jnp.float32),
+            pltpu.VMEM((tiles, ROW_TILE, LANES), jnp.float32),
             dma((spans, items)),
             dma((spans, items)),
             dma((2, heads)),

time: 72.6 us -> 70 us (0.964)
  Pallas kernels: 71.1 us -> 68.5 us
    pallas_call x1, Pallas kernels: 71.1 us -> 68.5 us  [on_device(): pl.pallas_call(functools.partial(fused, n, sections), out_shape=pltpu.VME...]
where the time goes in v4:
time: 70 us; the launch traced here: 69.8 us
  Pallas kernels  68.5 us (98%)
  local copies, waits for them, and re-layouts  1.32 us (2%)
    pallas_call x1, Pallas kernels, on_device(): pl.pallas_call(functools.partial(fused, n, sections), out_shape=pltpu.VME...  68.5 us

profile of v4, /device:TPU:0, one launch (start us, length us, event | category | flops | bytes accessed | tf_op | source)
XLA Modules:
  0.0 69.8 jit_solution(16689131848099197805)
XLA Ops:
  0.0 68.5 %shard_map.82 = bf16[1,2,128,4096]{3,2,1,0:T(8,128)(2,1)S(1)} custom-call(s32[2]{0:T(128)} %visible.1, s32[128,32]{1,0:T(8,128)} %bitcast.1, s32[1,4,2,16]{3,2,1,0:T(2,128)} %counts.1, bf16[1,2,128,4096]{3,2,1,0:T(8,128)(2,1)} %queries.1, bf16[1,2,128,1024]{3,2,1,0:T(8,128)(2,1)} %keys_new.1, bf16[1,2,128,1024]{3,2,1,0:T(8,128)(2,1)} %values_new.1, ...), custom_call_target="tpu_custom_call" | custom-call | tf_op jit(solution)/shard_map/pallas_call | solution.py:466
  68.5 1.3 %copy.10 = bf16[1,2,128,4096]{3,2,1,0:T(8,128)(2,1)} copy(bf16[1,2,128,4096]{3,2,1,0:T(8,128)(2,1)S(1)} %shard_map.82) | data formatting | bytes 4194304

commit v5 on v4

--- a/solution.py
+++ b/solution.py
@@ -46,9 +46,9 @@
 def fused(
     n,
     sections,
-    visible,
-    lists,
-    counts,
+    visible_in,
+    lists_in,
+    counts_in,
     queries,
     keys_new,
     values_new,
@@ -72,6 +72,10 @@
     stage,
     stage_recv,
     pass_send,
+    visible,
+    lists,
+    counts,
+    table_sem,
     gate,
 ):
     spans, heads, span_len = qbuf.shape[0], qbuf.shape[1], qbuf.shape[2]
@@ -166,6 +170,13 @@
         )
     pl.semaphore_wait(barrier, n + 1)
 
+    tables = [
+        pltpu.make_async_copy(there, here, table_sem.at[i])
+        for i, (there, here) in enumerate(
+            [(visible_in, visible), (lists_in, lists), (counts_in, counts)]
+        )
+    ]
+
     def send_items(span, some):
         for item in some:
 
@@ -179,6 +190,8 @@
 
     urgent = 1 + 2 * kv_dev
     send_items(0, order[:urgent])
+    for table in tables:
+        table.start()
 
     pl.semaphore_signal(gate, inc=1, device_id=(below, me), device_id_type=pl.DeviceIdType.MESH)
 
@@ -277,6 +290,8 @@
                 bias[j : j + 1, :], (BLK, columns)
             ).astype(jnp.bfloat16)
 
+    for table in tables:
+        table.wait()
     build_reach()
     pl.semaphore_wait(gate, 1)
 
@@ -456,7 +471,6 @@
     span_len = rows * n
     items = 2 * kv_dev + heads
     slots = block_lists.shape[4]
-    smem = pl.BlockSpec(memory_space=pltpu.MemorySpace.SMEM)
     vmem = pl.BlockSpec(memory_space=pltpu.MemorySpace.VMEM)
     anywhere = pl.BlockSpec(memory_space=pl.ANY)
     relayed = max(1, spans * heads - DIRECT)
@@ -466,7 +480,7 @@
     return pl.pallas_call(
         functools.partial(fused, n, sections),
         out_shape=pltpu.VMEM(queries.shape, queries.dtype),
-        in_specs=[smem, vmem, vmem] + [anywhere] * 5,
+        in_specs=[anywhere] * 8,
         out_specs=vmem,
         scratch_shapes=[
             pltpu.VMEM((spans, heads, span_len, DH), jnp.bfloat16),
@@ -486,6 +500,10 @@
             pltpu.VMEM((relayed, span_len, DH), jnp.bfloat16),
             dma((relayed,)),
             dma((1,)),
+            pltpu.SMEM(visible_blocks.shape, jnp.int32),
+            pltpu.VMEM((heads * spans * (span_len // BLK), slots), jnp.int32),
+            pltpu.VMEM(block_counts.shape, jnp.int32),
+            dma((3,)),
             pltpu.SemaphoreType.REGULAR,
         ],
         compiler_params=pltpu.CompilerParams(

time: 70 us -> 69 us (0.986)
  Pallas kernels: 68.5 us -> 67.6 us
    pallas_call x1, Pallas kernels: 68.5 us -> 67.6 us  [on_device(): pl.pallas_call(functools.partial(fused, n, sections), out_shape=pltpu.VME...]
where the time goes in v5:
time: 69 us; the launch traced here: 68.9 us
  Pallas kernels  67.6 us (98%)
  local copies, waits for them, and re-layouts  1.32 us (2%)
    pallas_call x1, Pallas kernels, on_device(): pl.pallas_call(functools.partial(fused, n, sections), out_shape=pltpu.VME...  67.6 us

profile of v5, /device:TPU:0, one launch (start us, length us, event | category | flops | bytes accessed | tf_op | source)
XLA Modules:
  0.0 68.9 jit_solution(4647047441269220598)
XLA Ops:
  0.0 67.6 %shard_map.82 = bf16[1,2,128,4096]{3,2,1,0:T(8,128)(2,1)S(1)} custom-call(s32[2]{0:T(128)} %visible_in.1, s32[128,32]{1,0:T(8,128)} %bitcast.1, s32[1,4,2,16]{3,2,1,0:T(2,128)} %counts_in.1, bf16[1,2,128,4096]{3,2,1,0:T(8,128)(2,1)} %queries.1, bf16[1,2,128,1024]{3,2,1,0:T(8,128)(2,1)} %keys_new.1, bf16[1,2,128,1024]{3,2,1,0:T(8,128)(2,1)} %values_new.1, ...), custom_call_target="tpu_custom_call" | custom-call | tf_op jit(solution)/shard_map/pallas_call | solution.py:480
  67.6 1.3 %copy.10 = bf16[1,2,128,4096]{3,2,1,0:T(8,128)(2,1)} copy(bf16[1,2,128,4096]{3,2,1,0:T(8,128)(2,1)S(1)} %shard_map.82) | data formatting | bytes 4194304

commit v6 on v5

--- a/solution.py
+++ b/solution.py
@@ -208,7 +208,7 @@
         return buffer.at[where, :], out.at[0, span, :, pl.ds(column, DH)]
 
     def out_copy(span, head, k):
-        seq_to = lax.rem(me + k, n)
+        seq_to = lax.rem(me + 2 + k, n)
         source_ref, target_ref = out_piece(att.at[span, head], span, head, me, seq_to)
         return mesh_copy(source_ref, target_ref, out_send.at[0], out_recv.at[0], above, seq_to)
 

time: 69 us -> 70.7 us (1.025)
  Pallas kernels: 67.6 us -> 69.2 us
    pallas_call x1, Pallas kernels: 67.6 us -> 69.2 us  [on_device(): pl.pallas_call(functools.partial(fused, n, sections), out_shape=pltpu.VME...]
where the time goes in v6:
time: 70.7 us; the launch traced here: 70.5 us
  Pallas kernels  69.2 us (98%)
  local copies, waits for them, and re-layouts  1.32 us (2%)
    pallas_call x1, Pallas kernels, on_device(): pl.pallas_call(functools.partial(fused, n, sections), out_shape=pltpu.VME...  69.2 us

profile of v6, /device:TPU:0, one launch (start us, length us, event | category | flops | bytes accessed | tf_op | source)
XLA Modules:
  0.0 70.5 jit_solution(10200443008633978975)
XLA Ops:
  0.0 69.2 %shard_map.82 = bf16[1,2,128,4096]{3,2,1,0:T(8,128)(2,1)S(1)} custom-call(s32[2]{0:T(128)} %visible_in.1, s32[128,32]{1,0:T(8,128)} %bitcast.1, s32[1,4,2,16]{3,2,1,0:T(2,128)} %counts_in.1, bf16[1,2,128,4096]{3,2,1,0:T(8,128)(2,1)} %queries.1, bf16[1,2,128,1024]{3,2,1,0:T(8,128)(2,1)} %keys_new.1, bf16[1,2,128,1024]{3,2,1,0:T(8,128)(2,1)} %values_new.1, ...), custom_call_target="tpu_custom_call" | custom-call | tf_op jit(solution)/shard_map/pallas_call | solution.py:480
  69.2 1.3 %copy.10 = bf16[1,2,128,4096]{3,2,1,0:T(8,128)(2,1)} copy(bf16[1,2,128,4096]{3,2,1,0:T(8,128)(2,1)S(1)} %shard_map.82) | data formatting | bytes 4194304
